TPU v7x, 32 devices: a whole 2x2x4 slice. The times are simulated.
32 devices in a mesh: section: 2 (over x), dp: 4 (over y, core), tensor: 4 (over z).
Axes of the slice: x: 2, y: 2, z: 4, core: 2. Of those that a mesh axis runs over, the one named last changes fastest.
Arguments:
- tokens: bfloat16 [8, 704, 768], P('dp', 'tensor'), may hold values from -6 to 6
- segment_ids: int32 [8, 704], P('dp'), may hold values from 0 to 3, as said below
- cotangent: bfloat16 [8, 704, 768], P('dp', 'tensor'), may hold values from -6 to 6
- norm_gain1: float32 [2, 768], P('section'), may hold values from 0.5 to 1.5
- w_in: bfloat16 [2, 768, 3, 768], P('section', None, None, 'tensor'), may hold values from -0.21875 to 0.21875
- short_taps: float32 [2, 3, 3, 768], P('section', None, None, 'tensor'), may hold values from -4 to 4
- cond_taps: float32 [2, 3, 768], P('section', None, 'tensor'), may hold values from -4 to 4
- spectrum: float32 [2, 2, 705, 768], P('section', None, None, 'tensor'), may hold values from -6 to 6
- spectral_gain: float32 [2, 2, 768], P('section', None, 'tensor'), may hold values from 0.3 to 3
- w_out: bfloat16 [2, 768, 768], P('section', 'tensor'), may hold values from -0.4375 to 0.4375
- norm_gain2: float32 [2, 768], P('section'), may hold values from 0.5 to 1.5
- w_gate_up: bfloat16 [2, 768, 2, 3072], P('section', None, None, 'tensor'), may hold values from -0.21875 to 0.21875
- w_down: bfloat16 [2, 3072, 768], P('section', 'tensor'), may hold values from -0.15625 to 0.15625
Outputs:
- layer_out: float32 [2, 8, 704, 768], P('section', 'dp', 'tensor')
- grad_in: float32 [2, 8, 704, 768], P('section', 'dp', 'tensor')
- grad_norm_gain1: float32 [2, 768], P('section')
- grad_w_in: float32 [2, 768, 3, 768], P('section', None, None, 'tensor')
- grad_short_taps: float32 [2, 3, 3, 768], P('section', None, None, 'tensor')
- grad_cond_taps: float32 [2, 3, 768], P('section', None, 'tensor')
- grad_spectrum: float32 [2, 2, 705, 768], P('section', None, None, 'tensor')
- grad_spectral_gain: float32 [2, 2, 768], P('section', None, 'tensor')
- grad_w_out: float32 [2, 768, 768], P('section', 'tensor')
- grad_norm_gain2: float32 [2, 768], P('section')
- grad_w_gate_up: float32 [2, 768, 2, 3072], P('section', None, None, 'tensor')
- grad_w_down: float32 [2, 3072, 768], P('section', 'tensor')
Inputs may be any that keep to these rules, and one draw needn't show every extreme that they name: `segment_ids`: in each pack the ids never fall along the rows, and each of the 4 ids holds one or more rows.
All inputs are finite; a program needn't handle non-finite values.
Results may differ from a plain program's by a relative error of at most 0.022.
The roundings to bfloat16 on the way count: a program that leaves them out, or rounds other values in their place, can miss the bound.
Values may be sent and summed in bfloat16 or wider, within the bound.
No kernel may reach another device: no remote copies, remote signals or barrier semaphores. Data moves between devices by JAX's collectives and lax.ppermute only.
A program may use at most 192 MiB of HBM per device.

v0:
```python
from functools import partial
import math
import jax
import jax.numpy as jnp
from jax import lax
from jax.sharding import PartitionSpec as P

SEGS = 4
highest = lax.Precision.HIGHEST


def from_behind(shard, axis, by):
    peers = lax.axis_size(axis)
    pairs = [(i, i + by) for i in range(peers) if 0 <= i + by < peers]
    return lax.ppermute(shard, axis, pairs)


def layer_norm(values, gain):
    row_mean = jnp.mean(values, axis=-1, keepdims=True)
    centred = values - row_mean
    variance = jnp.mean(centred * centred, axis=-1, keepdims=True)
    return centred * lax.rsqrt(variance + 1e-05) * gain


def neighbours(segments):
    equal = (segments[1:] == segments[:-1]).astype(jnp.float32)
    blank = jnp.zeros((1,), jnp.float32)
    return (jnp.concatenate([blank, equal]), jnp.concatenate([equal, blank]))


def masked_short(values, taps, same_prev, same_next):
    blank = jnp.zeros((1, values.shape[1]), values.dtype)
    before = jnp.concatenate([blank, values[:-1]], axis=0) * same_prev[:, None]
    after = jnp.concatenate([values[1:], blank], axis=0) * same_next[:, None]
    return taps[0] * before + taps[1] * values + taps[2] * after


def spectral_tables(pack_len):
    period = 2 * pack_len
    freq_index = lax.broadcasted_iota(jnp.int32, (pack_len + 1, pack_len), 0)
    place_index = lax.broadcasted_iota(jnp.int32, (pack_len + 1, pack_len), 1)
    angle = (freq_index * place_index % period).astype(jnp.float32) * (2.0 * math.pi / period)
    cosine = jnp.cos(angle)
    sine = jnp.sin(angle)
    forward_table = jnp.concatenate([cosine, -sine], axis=0)
    freq_column = freq_index[:, :1]
    column_weight = jnp.where((freq_column == 0) | (freq_column == pack_len), 1.0, 2.0) / period
    inverse_table = jnp.concatenate([cosine * column_weight, -sine * column_weight], axis=0).T
    return (forward_table, inverse_table)


def orchid_mix(proj, short_taps, cond_taps, spectrum, spectral_gain, segments, tables):
    forward_table, inverse_table = tables
    pack_len = proj.shape[0]
    channels = proj.shape[1] // 3
    freqs = pack_len + 1
    same_prev, same_next = neighbours(segments)
    shorted = masked_short(proj, short_taps, same_prev, same_next)
    query = shorted[:, :channels]
    key_part = shorted[:, channels : 2 * channels]
    value_part = shorted[:, 2 * channels :]
    condition = masked_short(key_part, cond_taps, same_prev, same_next)
    cond_hat = jnp.dot(forward_table, condition, precision=highest)
    scale_in = spectral_gain[0] / math.sqrt(pack_len)
    filt_re = spectrum[0] + spectral_gain[1] * jnp.tanh(scale_in * cond_hat[:freqs])
    filt_im = spectrum[1] + spectral_gain[1] * jnp.tanh(scale_in * cond_hat[freqs:])
    masks = (segments[:, None] == jnp.arange(SEGS, dtype=jnp.int32)[None, :]).astype(jnp.float32)
    pieces = (masks[:, :, None] * value_part[:, None, :]).reshape(pack_len, SEGS * channels)
    piece_hat = jnp.dot(forward_table, pieces, precision=highest).reshape(2, freqs, SEGS, channels)
    real_part = piece_hat[0] * filt_re[:, None, :] - piece_hat[1] * filt_im[:, None, :]
    imag_part = piece_hat[0] * filt_im[:, None, :] + piece_hat[1] * filt_re[:, None, :]
    joined = jnp.concatenate([real_part, imag_part], axis=0).reshape(2 * freqs, SEGS * channels)
    conv = jnp.dot(inverse_table, joined, precision=highest).reshape(pack_len, SEGS, channels)
    mixed = jnp.sum(conv * masks[:, :, None], axis=1)
    return query * mixed


def glu_act(both_parts):
    half_width = both_parts.shape[1] // 2
    return jax.nn.silu(both_parts[:, :half_width]) * both_parts[:, half_width:]


def mixer_local(gathered, segments, params, tables):
    (
        gain_one,
        w_in,
        short_taps,
        cond_taps,
        spectrum,
        spectral_gain,
        w_out,
        gain_two,
        w_gate_up,
        w_down,
    ) = params
    proj = jnp.dot(gathered, w_in, preferred_element_type=jnp.float32)
    mixer = partial(orchid_mix, segments=segments, tables=tables)
    mixed, mix_pull = jax.vjp(mixer, proj, short_taps, cond_taps, spectrum, spectral_gain)
    return (mixed.astype(jnp.bfloat16), mix_pull)


def glu_local(gathered_two, w_gate_up):
    both_parts = jnp.dot(gathered_two, w_gate_up, preferred_element_type=jnp.float32)
    act, act_pull = jax.vjp(glu_act, both_parts)
    return (act.astype(jnp.bfloat16), act_pull)


def run_layer(layer_input, segments, params, tables, finish):
    (
        gain_one,
        w_in,
        short_taps,
        cond_taps,
        spectrum,
        spectral_gain,
        w_out,
        gain_two,
        w_gate_up,
        w_down,
    ) = params
    normed, norm_pull = jax.vjp(layer_norm, layer_input, gain_one)
    gathered = lax.all_gather(normed.astype(jnp.bfloat16), "tensor", axis=0, tiled=True)
    mixed_low, mix_pull = mixer_local(gathered, segments, params, tables)
    hidden = layer_input + lax.psum_scatter(
        jnp.dot(mixed_low, w_out, preferred_element_type=jnp.float32),
        "tensor",
        scatter_dimension=0,
        tiled=True,
    )
    normed_two, norm_pull_two = jax.vjp(layer_norm, hidden, gain_two)
    gathered_two = lax.all_gather(normed_two.astype(jnp.bfloat16), "tensor", axis=0, tiled=True)
    act_low, act_pull = glu_local(gathered_two, w_gate_up)
    saved = (
        norm_pull,
        gathered,
        mixed_low,
        mix_pull,
        norm_pull_two,
        gathered_two,
        act_pull,
        act_low,
    )
    front_rows = (gathered, hidden, gathered_two)
    if finish:
        return (
            hidden
            + lax.psum_scatter(
                jnp.dot(act_low, w_down, preferred_element_type=jnp.float32),
                "tensor",
                scatter_dimension=0,
                tiled=True,
            ),
            saved,
            front_rows,
        )
    return (hidden, saved, front_rows)


def back_layer(layer_input, segments, params, tables, grad_out):
    (
        gain_one,
        w_in,
        short_taps,
        cond_taps,
        spectrum,
        spectral_gain,
        w_out,
        gain_two,
        w_gate_up,
        w_down,
    ) = params
    hidden, saved, front_rows = run_layer(layer_input, segments, params, tables, False)
    norm_pull, gathered, mixed_low, mix_pull, norm_pull_two, gathered_two, act_pull, act_low = saved
    grad_rows = lax.all_gather(grad_out.astype(jnp.bfloat16), "tensor", axis=0, tiled=True)
    grad_act = jnp.einsum("ld,fd->lf", grad_rows, w_down, preferred_element_type=jnp.float32)
    grad_down = jnp.einsum("lf,ld->fd", act_low, grad_rows, preferred_element_type=jnp.float32)
    grad_both = act_pull(grad_act)[0].astype(jnp.bfloat16)
    grad_gate_up = jnp.einsum(
        "ld,lf->df", gathered_two, grad_both, preferred_element_type=jnp.float32
    )
    piece = grad_both
    grad_normed_two = lax.psum_scatter(
        jnp.einsum("lf,df->ld", piece, w_gate_up, preferred_element_type=jnp.float32),
        "tensor",
        scatter_dimension=0,
        tiled=True,
    )
    grad_hidden_part, grad_gain_two = norm_pull_two(grad_normed_two)
    grad_hidden = grad_out + grad_hidden_part
    grad_mix_rows = lax.all_gather(grad_hidden.astype(jnp.bfloat16), "tensor", axis=0, tiled=True)
    grad_mixed = jnp.einsum("ld,cd->lc", grad_mix_rows, w_out, preferred_element_type=jnp.float32)
    grad_w_out = jnp.einsum(
        "lc,ld->cd", mixed_low, grad_mix_rows, preferred_element_type=jnp.float32
    )
    grad_proj, grad_short, grad_cond, grad_spectrum, grad_spectral = mix_pull(grad_mixed)
    grad_proj_low = grad_proj.astype(jnp.bfloat16)
    grad_w_in = jnp.einsum("ld,lc->dc", gathered, grad_proj_low, preferred_element_type=jnp.float32)
    piece = grad_proj_low
    grad_normed = lax.psum_scatter(
        jnp.einsum("lc,dc->ld", piece, w_in, preferred_element_type=jnp.float32),
        "tensor",
        scatter_dimension=0,
        tiled=True,
    )
    grad_input_part, grad_gain_one = norm_pull(grad_normed)
    grad_input = grad_hidden + grad_input_part
    weight_terms = (
        grad_w_in,
        grad_short,
        grad_cond,
        grad_spectrum,
        grad_spectral,
        grad_w_out,
        grad_gate_up,
        grad_down,
    )
    return (grad_input, (grad_gain_one, grad_gain_two), weight_terms)


def per_device(
    tokens,
    segment_ids,
    cotangent,
    norm_gain1,
    w_in,
    short_taps,
    cond_taps,
    spectrum,
    spectral_gain,
    w_out,
    norm_gain2,
    w_gate_up,
    w_down,
):
    pack_count, row_count, model_width = tokens.shape
    pack_len = segment_ids.shape[1]
    channels = w_in.shape[3]
    hidden_cols = w_gate_up.shape[3]
    params = (
        norm_gain1[0],
        w_in[0].reshape(model_width, 3 * channels),
        short_taps[0].reshape(3, 3 * channels),
        cond_taps[0],
        spectrum[0],
        spectral_gain[0],
        w_out[0],
        norm_gain2[0],
        w_gate_up[0].reshape(model_width, 2 * hidden_cols),
        w_down[0],
    )
    tables = spectral_tables(pack_len)
    section_index = lax.axis_index("section")
    last_section = lax.axis_size("section") - 1
    step_count = pack_count + last_section

    def forward_step(loop_state, step_index):
        sent, kept_in, kept_out, kept_extra = loop_state
        received = from_behind(sent, "section", 1)
        micro = step_index - section_index
        is_valid = (micro >= 0) & (micro < pack_count)
        slot_index = jnp.clip(micro, 0, pack_count - 1)
        own_rows = lax.dynamic_index_in_dim(tokens, slot_index, 0, keepdims=False).astype(
            jnp.float32
        )
        layer_input = jnp.where(section_index == 0, own_rows, received)
        segments = lax.dynamic_index_in_dim(segment_ids, slot_index, 0, keepdims=False)
        result, unused_saved, front_rows = run_layer(layer_input, segments, params, tables, True)
        kept_in = jnp.where(
            is_valid, lax.dynamic_update_index_in_dim(kept_in, layer_input, slot_index, 0), kept_in
        )
        kept_out = jnp.where(
            is_valid, lax.dynamic_update_index_in_dim(kept_out, result, slot_index, 0), kept_out
        )
        return ((result, kept_in, kept_out, kept_extra), None)

    extra_start = ()
    start_state = (
        jnp.zeros((row_count, model_width), jnp.float32),
        jnp.zeros((pack_count, row_count, model_width), jnp.float32),
        jnp.zeros((pack_count, row_count, model_width), jnp.float32),
        extra_start,
    )
    (unused_rows, kept_in, kept_out, kept_extra), unused_steps = lax.scan(
        forward_step, start_state, jnp.arange(step_count)
    )
    weight_shapes = (
        params[1],
        params[2],
        params[3],
        params[4],
        params[5],
        params[6],
        params[8],
        params[9],
    )
    zero_weights = tuple((jnp.zeros(array.shape, jnp.float32) for array in weight_shapes))
    zero_gains = (jnp.zeros((model_width,), jnp.float32), jnp.zeros((model_width,), jnp.float32))

    def backward_step(loop_state, step_index):
        sent, kept_grad, gain_totals, weight_totals = loop_state
        received = from_behind(sent, "section", -1)
        micro = step_index - (last_section - section_index)
        is_valid = (micro >= 0) & (micro < pack_count)
        slot_index = jnp.clip(micro, 0, pack_count - 1)
        own_grad = lax.dynamic_index_in_dim(cotangent, slot_index, 0, keepdims=False).astype(
            jnp.float32
        )
        grad_out = jnp.where(section_index == last_section, own_grad, received)
        layer_input = lax.dynamic_index_in_dim(kept_in, slot_index, 0, keepdims=False)
        segments = lax.dynamic_index_in_dim(segment_ids, slot_index, 0, keepdims=False)
        grad_input, gain_terms, weight_terms = back_layer(
            layer_input, segments, params, tables, grad_out
        )
        gain_terms = tuple((jnp.where(is_valid, term, 0.0) for term in gain_terms))
        term_in, term_short, term_cond, term_spec, term_gain, term_out, term_gate_up, term_down = (
            tuple((jnp.where(is_valid, term, 0.0) for term in weight_terms))
        )
        new_terms = (
            term_in,
            term_short,
            term_cond,
            term_spec,
            term_gain,
            term_out,
            term_gate_up,
            term_down,
        )
        weight_totals = tuple((total + term for total, term in zip(weight_totals, new_terms)))
        gain_totals = tuple((total + term for total, term in zip(gain_totals, gain_terms)))
        kept_grad = jnp.where(
            is_valid,
            lax.dynamic_update_index_in_dim(kept_grad, grad_input, slot_index, 0),
            kept_grad,
        )
        return ((grad_input, kept_grad, gain_totals, weight_totals), None)

    back_start = (
        jnp.zeros((row_count, model_width), jnp.float32),
        jnp.zeros((pack_count, row_count, model_width), jnp.float32),
        zero_gains,
        zero_weights,
    )
    (unused_grad, kept_grad, gain_totals, weight_totals), unused_back = lax.scan(
        backward_step, back_start, jnp.arange(step_count)
    )
    sum_in, sum_short, sum_cond, sum_spec, sum_gain, sum_out, sum_gate_up, sum_down = weight_totals
    sum_in, sum_short, sum_cond, sum_spec, sum_gain, sum_out, sum_gate_up, sum_down = lax.psum(
        (sum_in, sum_short, sum_cond, sum_spec, sum_gain, sum_out, sum_gate_up, sum_down), "dp"
    )
    gain_first, gain_second = gain_totals
    gain_first, gain_second = lax.psum((gain_first, gain_second), ("dp", "tensor"))
    return (
        kept_out[None],
        kept_grad[None],
        gain_first[None],
        sum_in.reshape(1, model_width, 3, channels),
        sum_short.reshape(1, 3, 3, channels),
        sum_cond[None],
        sum_spec[None],
        sum_gain[None],
        sum_out[None],
        gain_second[None],
        sum_gate_up.reshape(1, model_width, 2, hidden_cols),
        sum_down[None],
    )


def solution(mesh):
    return jax.shard_map(
        per_device,
        mesh=mesh,
        in_specs=(
            P("dp", "tensor", None),
            P("dp", None),
            P("dp", "tensor", None),
            P("section", None),
            P("section", None, None, "tensor"),
            P("section", None, None, "tensor"),
            P("section", None, "tensor"),
            P("section", None, None, "tensor"),
            P("section", None, "tensor"),
            P("section", "tensor", None),
            P("section", None),
            P("section", None, None, "tensor"),
            P("section", "tensor", None),
        ),
        out_specs=(
            P("section", "dp", "tensor", None),
            P("section", "dp", "tensor", None),
            P("section", None),
            P("section", None, None, "tensor"),
            P("section", None, None, "tensor"),
            P("section", None, "tensor"),
            P("section", None, None, "tensor"),
            P("section", None, "tensor"),
            P("section", "tensor", None),
            P("section", None),
            P("section", None, None, "tensor"),
            P("section", "tensor", None),
        ),
        check_vma=False,
    )
```

profile of v0, /device:TPU:0, one launch (start us, length us, event | category | flops | bytes accessed | tf_op | source)
XLA Modules:
  0.0 2237.0 jit_solution(2906031752056489237)
XLA Ops:
  48.2 704.4 %while.51 = (s32[]{:T(128)}, f32[176,768]{1,0:T(8,128)S(1)}, f32[2,176,768]{2,1,0:T(8,128)S(1)}, f32[2,176,768]{2,1,0:T(8,128)}, pred[]{:T(512)}, /*index=5*/s32...) while((s32[]{:T(128)}, f32[176,768]{1,0:T(8,128)S(1)}, ...), condition=%wide.region_8.9_spmd.clone, body=%wide.region_0.8_spmd.clone.sunk | while | flops 23922319360 | bytes 190306960 | solution.py:283
  67.5 30.6 %all-gather.7.cloned.1.call-done = bf16[704,768]{1,0:T(8,128)(2,1)} async-done(((bf16[176,768]{1,0:T(8,128)(2,1)}), bf16[704,768]{1,0:T(8,128)(2,1)}) %all-gather.7.cloned.1.call-update) | async-done | bytes 1081360 | tf_op jit(solution)/shard_map/while/body/eval_jaxpr/all_gather | solution.py:122
  113.5 13.8 convolution_bitcast_fusion.15
  136.2 13.8 fusion.255
  157.9 43.8 %reduce-scatter.6.cloned.1.call-done = f32[176,768]{1,0:T(8,128)} async-done(((f32[704,768]{1,0:T(8,128)}), f32[176,768]{1,0:T(8,128)}) %reduce-scatter.6.cloned.1.call-update) | async-done | bytes 540688 | tf_op jit(solution)/shard_map/while/body/eval_jaxpr/reduce_scatter | solution.py:124
  204.0 28.0 %all-gather.9.cloned.1.call-done = bf16[704,768]{1,0:T(8,128)(2,1)} async-done(((bf16[176,768]{1,0:T(8,128)(2,1)}), bf16[704,768]{1,0:T(8,128)(2,1)}) %all-gather.9.cloned.1.call-update) | async-done | bytes 1081360 | tf_op jit(solution)/shard_map/while/body/eval_jaxpr/all_gather | solution.py:131
  238.6 44.6 %reduce-scatter.8.cloned.1.call-done = f32[176,768]{1,0:T(8,128)} async-done(((f32[704,768]{1,0:T(8,128)}), f32[176,768]{1,0:T(8,128)}) %reduce-scatter.8.cloned.1.call-update) | async-done | bytes 540688 | tf_op jit(solution)/shard_map/while/body/eval_jaxpr/reduce_scatter | solution.py:147
  302.8 28.9 %all-gather.7.cloned.1.call-done = bf16[704,768]{1,0:T(8,128)(2,1)} async-done(((bf16[176,768]{1,0:T(8,128)(2,1)}), bf16[704,768]{1,0:T(8,128)(2,1)}) %all-gather.7.cloned.1.call-update) | async-done | bytes 1081360 | tf_op jit(solution)/shard_map/while/body/eval_jaxpr/all_gather | solution.py:122
  347.1 13.8 convolution_bitcast_fusion.15
  369.8 13.8 fusion.255
  391.5 43.8 %reduce-scatter.6.cloned.1.call-done = f32[176,768]{1,0:T(8,128)} async-done(((f32[704,768]{1,0:T(8,128)}), f32[176,768]{1,0:T(8,128)}) %reduce-scatter.6.cloned.1.call-update) | async-done | bytes 540688 | tf_op jit(solution)/shard_map/while/body/eval_jaxpr/reduce_scatter | solution.py:124
  437.7 28.0 %all-gather.9.cloned.1.call-done = bf16[704,768]{1,0:T(8,128)(2,1)} async-done(((bf16[176,768]{1,0:T(8,128)(2,1)}), bf16[704,768]{1,0:T(8,128)(2,1)}) %all-gather.9.cloned.1.call-update) | async-done | bytes 1081360 | tf_op jit(solution)/shard_map/while/body/eval_jaxpr/all_gather | solution.py:131
  472.2 44.6 %reduce-scatter.8.cloned.1.call-done = f32[176,768]{1,0:T(8,128)} async-done(((f32[704,768]{1,0:T(8,128)}), f32[176,768]{1,0:T(8,128)}) %reduce-scatter.8.cloned.1.call-update) | async-done | bytes 540688 | tf_op jit(solution)/shard_map/while/body/eval_jaxpr/reduce_scatter | solution.py:147
  536.4 28.9 %all-gather.7.cloned.1.call-done = bf16[704,768]{1,0:T(8,128)(2,1)} async-done(((bf16[176,768]{1,0:T(8,128)(2,1)}), bf16[704,768]{1,0:T(8,128)(2,1)}) %all-gather.7.cloned.1.call-update) | async-done | bytes 1081360 | tf_op jit(solution)/shard_map/while/body/eval_jaxpr/all_gather | solution.py:122
  603.4 13.8 fusion.255
  625.1 43.8 %reduce-scatter.6.cloned.1.call-done = f32[176,768]{1,0:T(8,128)} async-done(((f32[704,768]{1,0:T(8,128)}), f32[176,768]{1,0:T(8,128)}) %reduce-scatter.6.cloned.1.call-update) | async-done | bytes 540688 | tf_op jit(solution)/shard_map/while/body/eval_jaxpr/reduce_scatter | solution.py:124
  671.3 28.0 %all-gather.9.cloned.1.call-done = bf16[704,768]{1,0:T(8,128)(2,1)} async-done(((bf16[176,768]{1,0:T(8,128)(2,1)}), bf16[704,768]{1,0:T(8,128)(2,1)}) %all-gather.9.cloned.1.call-update) | async-done | bytes 1081360 | tf_op jit(solution)/shard_map/while/body/eval_jaxpr/all_gather | solution.py:131
  705.8 44.6 %reduce-scatter.8.cloned.1.call-done = f32[176,768]{1,0:T(8,128)} async-done(((f32[704,768]{1,0:T(8,128)}), f32[176,768]{1,0:T(8,128)}) %reduce-scatter.8.cloned.1.call-update) | async-done | bytes 540688 | tf_op jit(solution)/shard_map/while/body/eval_jaxpr/reduce_scatter | solution.py:147
  753.6 1268.6 %while.52 = (s32[]{:T(128)}, f32[176,768]{1,0:T(8,128)}, f32[2,176,768]{2,1,0:T(8,128)}, f32[768]{0:T(1024)}, f32[768]{0:T(1024)}, /*index=5*/f32[768,576]{0,1:T...) while((s32[]{:T(128)}, f32[176,768]{1,0:T(8,128)}, ...), condition=%wide.region_39.40_spmd.clone, body=%wide.region_9.39_spmd.clone.sunk | while | flops 50368700416 | bytes 605911616 | solution.py:343
  759.0 25.9 %all-gather.11.cloned.1.call-done = bf16[704,768]{1,0:T(8,128)(2,1)} async-done(((bf16[176,768]{1,0:T(8,128)(2,1)}), bf16[704,768]{1,0:T(8,128)(2,1)}) %all-gather.11.cloned.1.call-update) | async-done | bytes 1081360 | tf_op jit(solution)/shard_map/while/body/eval_jaxpr/all_gather | solution.py:122
  826.6 13.9 fusion.299
  850.3 43.2 %reduce-scatter.10.cloned.1.call-done = f32[176,768]{1,0:T(8,128)} async-done(((f32[704,768]{1,0:T(8,128)}), f32[176,768]{1,0:T(8,128)}) %reduce-scatter.10.cloned.1.call-update) | async-done | bytes 540688 | tf_op jit(solution)/shard_map/while/body/eval_jaxpr/reduce_scatter | solution.py:124
  898.6 14.5 collective-permute-done.1
  931.1 23.5 %all-gather.15.cloned.1.call-done = bf16[704,768]{1,0:T(8,128)(2,1)} async-done(((bf16[176,768]{1,0:T(8,128)(2,1)}), bf16[704,768]{1,0:T(8,128)(2,1)}) %all-gather.15.cloned.1.call-update) | async-done | bytes 1081360 | tf_op jit(solution)/shard_map/while/body/eval_jaxpr/all_gather | solution.py:174
  964.5 44.5 %reduce-scatter.12.cloned.1.call-done = f32[176,768]{1,0:T(8,128)} async-done(((f32[704,768]{1,0:T(8,128)}), f32[176,768]{1,0:T(8,128)}) %reduce-scatter.12.cloned.1.call-update) | async-done | bytes 540688 | tf_op jit(solution)/shard_map/while/body/eval_jaxpr/reduce_scatter | solution.py:182
  1023.1 20.0 all-gather.17.cloned.1.call-done
  1085.0 14.8 convolution_bitcast_fusion.20
  1144.2 26.5 %reduce-scatter.14.cloned.1.call-done = f32[176,768]{1,0:T(8,128)} async-done(((f32[704,768]{1,0:T(8,128)}), f32[176,768]{1,0:T(8,128)}) %reduce-scatter.14.cloned.1.call-update) | async-done | bytes 540688 | tf_op jit(solution)/shard_map/while/body/eval_jaxpr/reduce_scatter | solution.py:199
  1181.1 25.9 %all-gather.11.cloned.1.call-done = bf16[704,768]{1,0:T(8,128)(2,1)} async-done(((bf16[176,768]{1,0:T(8,128)(2,1)}), bf16[704,768]{1,0:T(8,128)(2,1)}) %all-gather.11.cloned.1.call-update) | async-done | bytes 1081360 | tf_op jit(solution)/shard_map/while/body/eval_jaxpr/all_gather | solution.py:122
  1248.6 13.9 fusion.299
  1272.3 43.3 %reduce-scatter.10.cloned.1.call-done = f32[176,768]{1,0:T(8,128)} async-done(((f32[704,768]{1,0:T(8,128)}), f32[176,768]{1,0:T(8,128)}) %reduce-scatter.10.cloned.1.call-update) | async-done | bytes 540688 | tf_op jit(solution)/shard_map/while/body/eval_jaxpr/reduce_scatter | solution.py:124
  1321.7 14.4 collective-permute-done.1
  1353.2 23.7 %all-gather.15.cloned.1.call-done = bf16[704,768]{1,0:T(8,128)(2,1)} async-done(((bf16[176,768]{1,0:T(8,128)(2,1)}), bf16[704,768]{1,0:T(8,128)(2,1)}) %all-gather.15.cloned.1.call-update) | async-done | bytes 1081360 | tf_op jit(solution)/shard_map/while/body/eval_jaxpr/all_gather | solution.py:174
  1386.7 44.5 %reduce-scatter.12.cloned.1.call-done = f32[176,768]{1,0:T(8,128)} async-done(((f32[704,768]{1,0:T(8,128)}), f32[176,768]{1,0:T(8,128)}) %reduce-scatter.12.cloned.1.call-update) | async-done | bytes 540688 | tf_op jit(solution)/shard_map/while/body/eval_jaxpr/reduce_scatter | solution.py:182
  1445.3 20.0 all-gather.17.cloned.1.call-done
  1507.2 14.8 convolution_bitcast_fusion.20
  1569.3 23.5 %reduce-scatter.14.cloned.1.call-done = f32[176,768]{1,0:T(8,128)} async-done(((f32[704,768]{1,0:T(8,128)}), f32[176,768]{1,0:T(8,128)}) %reduce-scatter.14.cloned.1.call-update) | async-done | bytes 540688 | tf_op jit(solution)/shard_map/while/body/eval_jaxpr/reduce_scatter | solution.py:199
  1603.3 25.9 %all-gather.11.cloned.1.call-done = bf16[704,768]{1,0:T(8,128)(2,1)} async-done(((bf16[176,768]{1,0:T(8,128)(2,1)}), bf16[704,768]{1,0:T(8,128)(2,1)}) %all-gather.11.cloned.1.call-update) | async-done | bytes 1081360 | tf_op jit(solution)/shard_map/while/body/eval_jaxpr/all_gather | solution.py:122
  1670.8 13.9 fusion.299
  1694.5 43.2 %reduce-scatter.10.cloned.1.call-done = f32[176,768]{1,0:T(8,128)} async-done(((f32[704,768]{1,0:T(8,128)}), f32[176,768]{1,0:T(8,128)}) %reduce-scatter.10.cloned.1.call-update) | async-done | bytes 540688 | tf_op jit(solution)/shard_map/while/body/eval_jaxpr/reduce_scatter | solution.py:124
  1743.9 14.5 collective-permute-done.1
  1775.4 23.5 %all-gather.15.cloned.1.call-done = bf16[704,768]{1,0:T(8,128)(2,1)} async-done(((bf16[176,768]{1,0:T(8,128)(2,1)}), bf16[704,768]{1,0:T(8,128)(2,1)}) %all-gather.15.cloned.1.call-update) | async-done | bytes 1081360 | tf_op jit(solution)/shard_map/while/body/eval_jaxpr/all_gather | solution.py:174
  1808.7 44.5 %reduce-scatter.12.cloned.1.call-done = f32[176,768]{1,0:T(8,128)} async-done(((f32[704,768]{1,0:T(8,128)}), f32[176,768]{1,0:T(8,128)}) %reduce-scatter.12.cloned.1.call-update) | async-done | bytes 540688 | tf_op jit(solution)/shard_map/while/body/eval_jaxpr/reduce_scatter | solution.py:182
  1867.3 20.0 all-gather.17.cloned.1.call-done
  1929.2 14.8 convolution_bitcast_fusion.20
  1991.4 23.5 %reduce-scatter.14.cloned.1.call-done = f32[176,768]{1,0:T(8,128)} async-done(((f32[704,768]{1,0:T(8,128)}), f32[176,768]{1,0:T(8,128)}) %reduce-scatter.14.cloned.1.call-update) | async-done | bytes 540688 | tf_op jit(solution)/shard_map/while/body/eval_jaxpr/reduce_scatter | solution.py:199
  2029.7 33.8 %all-reduce.34 = (f32[1,768]{1,0:T(1,128)}, f32[1,768]{1,0:T(1,128)}) all-reduce(f32[1,768]{1,0:T(1,128)S(1)} %broadcast_in_dim.232, f32[1,768]{1,0:T(1,128)S(1)} %broadcast_in_dim.237), channel_id=1, replica_groups=mesh['section'=2,'dp'=4,'tensor'=4] {'dp','tensor'}, use_global_device_ids=true, to_apply=%region_40.41 | all-reduce | flops 1536 | bytes 12288 | tf_op jit(solution)/shard_map/psum | solution.py:351
  2075.9 143.5 %all-reduce.39.cloned.1.call-done = (f32[1,768,3,192]{1,3,2,0:T(8,128)}, f32[1,2,705,192]{2,3,1,0:T(8,128)}, f32[1,192,768]{2,1,0:T(8,128)}, f32[1,768,2,768]{3,2,1,0:T(2,128)}, f32[1,768,768]{2,1,0:T(8,128)}) async-done(((f32[1,768,3,192]{1,3,2,0:T(8,128)}, f32[1,2,705,192]{2,3,1,0:T(8,128)}, f32[1,192,768]{2,1,0:T(8,128)}, f32[1,768,2,768]{3,2,1,0:T(2,128)}, f32[1,768,768]{2,1,0:T(8,128)}), ...) | async-done | bytes 10520080 | tf_op jit(solution)/shard_map/psum | solution.py:347
  (1307 shorter events, 848.8 us)
Async XLA Ops:
  48.4 49.6 %all-gather.7.cloned.1.call-start = ((), (), s32[]{:S(2)}) async-start(), calls=%async_computation.6 | async-start | bytes 1351680 | tf_op jit(solution)/shard_map/while/body/eval_jaxpr/all_gather | solution.py:122
  48.5 16.4 collective-permute-start
  67.2 134.5 %reduce-scatter.6.cloned.1.call-start = ((), (), s32[]{:S(2)}) async-start(), calls=%async_computation.7 | async-start | bytes 2703360 | tf_op jit(solution)/shard_map/while/body/eval_jaxpr/reduce_scatter | solution.py:124
  157.1 74.9 %all-gather.9.cloned.1.call-start = ((), (), s32[]{:S(2)}) async-start(), calls=%async_computation.8 | async-start | bytes 1351680 | tf_op jit(solution)/shard_map/while/body/eval_jaxpr/all_gather | solution.py:131
  204.0 79.2 %reduce-scatter.8.cloned.1.call-start = ((), (), s32[]{:S(2)}) async-start(), calls=%async_computation.9 | async-start | bytes 2703360 | tf_op jit(solution)/shard_map/while/body/eval_jaxpr/reduce_scatter | solution.py:147
  238.6 44.6 %copy-start.42 = (f32[2,176,768]{2,1,0:T(8,128)S(1)}, f32[2,176,768]{2,1,0:T(8,128)}, u32[]{:S(2)}) copy-start(f32[2,176,768]{2,1,0:T(8,128)} %get-tuple-element.1576) | copy-start | bytes 3244036 | tf_op jit(solution)/shard_map/while
  285.4 46.3 %all-gather.7.cloned.1.call-start = ((), (), s32[]{:S(2)}) async-start(), calls=%async_computation.6 | async-start | bytes 1351680 | tf_op jit(solution)/shard_map/while/body/eval_jaxpr/all_gather | solution.py:122
  285.4 14.7 collective-permute-start
  302.5 132.9 %reduce-scatter.6.cloned.1.call-start = ((), (), s32[]{:S(2)}) async-start(), calls=%async_computation.7 | async-start | bytes 2703360 | tf_op jit(solution)/shard_map/while/body/eval_jaxpr/reduce_scatter | solution.py:124
  390.7 74.9 %all-gather.9.cloned.1.call-start = ((), (), s32[]{:S(2)}) async-start(), calls=%async_computation.8 | async-start | bytes 1351680 | tf_op jit(solution)/shard_map/while/body/eval_jaxpr/all_gather | solution.py:131
  437.6 79.2 %reduce-scatter.8.cloned.1.call-start = ((), (), s32[]{:S(2)}) async-start(), calls=%async_computation.9 | async-start | bytes 2703360 | tf_op jit(solution)/shard_map/while/body/eval_jaxpr/reduce_scatter | solution.py:147
  472.2 44.6 %copy-start.42 = (f32[2,176,768]{2,1,0:T(8,128)S(1)}, f32[2,176,768]{2,1,0:T(8,128)}, u32[]{:S(2)}) copy-start(f32[2,176,768]{2,1,0:T(8,128)} %get-tuple-element.1576) | copy-start | bytes 3244036 | tf_op jit(solution)/shard_map/while
  519.0 46.3 %all-gather.7.cloned.1.call-start = ((), (), s32[]{:S(2)}) async-start(), calls=%async_computation.6 | async-start | bytes 1351680 | tf_op jit(solution)/shard_map/while/body/eval_jaxpr/all_gather | solution.py:122
  519.0 14.7 collective-permute-start
  536.1 132.9 %reduce-scatter.6.cloned.1.call-start = ((), (), s32[]{:S(2)}) async-start(), calls=%async_computation.7 | async-start | bytes 2703360 | tf_op jit(solution)/shard_map/while/body/eval_jaxpr/reduce_scatter | solution.py:124
  624.3 74.9 %all-gather.9.cloned.1.call-start = ((), (), s32[]{:S(2)}) async-start(), calls=%async_computation.8 | async-start | bytes 1351680 | tf_op jit(solution)/shard_map/while/body/eval_jaxpr/all_gather | solution.py:131
  671.2 79.2 %reduce-scatter.8.cloned.1.call-start = ((), (), s32[]{:S(2)}) async-start(), calls=%async_computation.9 | async-start | bytes 2703360 | tf_op jit(solution)/shard_map/while/body/eval_jaxpr/reduce_scatter | solution.py:147
  705.8 44.6 %copy-start.42 = (f32[2,176,768]{2,1,0:T(8,128)S(1)}, f32[2,176,768]{2,1,0:T(8,128)}, u32[]{:S(2)}) copy-start(f32[2,176,768]{2,1,0:T(8,128)} %get-tuple-element.1576) | copy-start | bytes 3244036 | tf_op jit(solution)/shard_map/while
  754.1 33.3 %copy-start.5 = (f32[2,176,768]{2,1,0:T(8,128)}, f32[2,176,768]{2,1,0:T(8,128)S(1)}, u32[]{:S(2)}) copy-start(f32[2,176,768]{2,1,0:T(8,128)S(1)} %get-tuple-element.1720) | copy-start | bytes 3244036 | tf_op jit(solution)/shard_map/while
  754.1 33.3 %copy-start.59 = (s32[2,704]{1,0:T(2,128)}, s32[2,704]{1,0:T(2,128)S(1)}, u32[]{:S(2)}) copy-start(s32[2,704]{1,0:T(2,128)S(1)} %get-tuple-element.1724) | copy-start | bytes 16900 | tf_op jit(solution)/shard_map/while
  754.1 33.3 %copy-start.86 = (f32[1,768]{1,0:T(1,128)}, f32[1,768]{1,0:T(1,128)S(1)}, u32[]{:S(2)}) copy-start(f32[1,768]{1,0:T(1,128)S(1)} %get-tuple-element.1722) | copy-start | bytes 9220 | tf_op jit(solution)/shard_map/while
  754.1 33.3 %copy-start.88 = (f32[3,192]{1,0:T(4,128)}, f32[3,192]{1,0:T(4,128)S(1)}, u32[]{:S(2)}) copy-start(f32[3,192]{1,0:T(4,128)S(1)} %get-tuple-element.1728) | copy-start | bytes 6916 | tf_op jit(solution)/shard_map/while
  754.2 30.8 %all-gather.11.cloned.1.call-start = ((), (), s32[]{:S(2)}) async-start(), calls=%async_computation.10 | async-start | bytes 1351680 | tf_op jit(solution)/shard_map/while/body/eval_jaxpr/all_gather | solution.py:122
  756.9 136.6 %reduce-scatter.10.cloned.1.call-start = ((), (), s32[]{:S(2)}) async-start(), calls=%async_computation.11 | async-start | bytes 2703360 | tf_op jit(solution)/shard_map/while/body/eval_jaxpr/reduce_scatter | solution.py:124
  849.0 76.2 %all-gather.13.cloned.1.call-start = ((), (), s32[]{:S(2)}) async-start(), calls=%async_computation.12 | async-start | bytes 1351680 | tf_op jit(solution)/shard_map/while/body/eval_jaxpr/all_gather | solution.py:131
  897.2 57.4 %all-gather.15.cloned.1.call-start = ((), (), s32[]{:S(2)}) async-start(), calls=%async_computation.13 | async-start | bytes 1351680 | tf_op jit(solution)/shard_map/while/body/eval_jaxpr/all_gather | solution.py:174
  897.3 15.8 collective-permute-start.1
  915.6 93.4 %reduce-scatter.12.cloned.1.call-start = ((), (), s32[]{:S(2)}) async-start(), calls=%async_computation.14 | async-start | bytes 2703360 | tf_op jit(solution)/shard_map/while/body/eval_jaxpr/reduce_scatter | solution.py:182
  964.5 78.6 %all-gather.17.cloned.1.call-start = ((), (), s32[]{:S(2)}) async-start(), calls=%async_computation.15 | async-start | bytes 1351680 | tf_op jit(solution)/shard_map/while/body/eval_jaxpr/all_gather | solution.py:190
  1015.1 155.6 %reduce-scatter.14.cloned.1.call-start = ((), (), s32[]{:S(2)}) async-start(), calls=%async_computation.16 | async-start | bytes 2703360 | tf_op jit(solution)/shard_map/while/body/eval_jaxpr/reduce_scatter | solution.py:199
  1176.2 30.7 %all-gather.11.cloned.1.call-start = ((), (), s32[]{:S(2)}) async-start(), calls=%async_computation.10 | async-start | bytes 1351680 | tf_op jit(solution)/shard_map/while/body/eval_jaxpr/all_gather | solution.py:122
  1179.0 136.6 %reduce-scatter.10.cloned.1.call-start = ((), (), s32[]{:S(2)}) async-start(), calls=%async_computation.11 | async-start | bytes 2703360 | tf_op jit(solution)/shard_map/while/body/eval_jaxpr/reduce_scatter | solution.py:124
  1271.0 76.3 %all-gather.13.cloned.1.call-start = ((), (), s32[]{:S(2)}) async-start(), calls=%async_computation.12 | async-start | bytes 1351680 | tf_op jit(solution)/shard_map/while/body/eval_jaxpr/all_gather | solution.py:131
  1319.3 57.6 %all-gather.15.cloned.1.call-start = ((), (), s32[]{:S(2)}) async-start(), calls=%async_computation.13 | async-start | bytes 1351680 | tf_op jit(solution)/shard_map/while/body/eval_jaxpr/all_gather | solution.py:174
  1320.4 15.8 collective-permute-start.1
  1338.7 92.5 %reduce-scatter.12.cloned.1.call-start = ((), (), s32[]{:S(2)}) async-start(), calls=%async_computation.14 | async-start | bytes 2703360 | tf_op jit(solution)/shard_map/while/body/eval_jaxpr/reduce_scatter | solution.py:182
  1386.6 78.6 %all-gather.17.cloned.1.call-start = ((), (), s32[]{:S(2)}) async-start(), calls=%async_computation.15 | async-start | bytes 1351680 | tf_op jit(solution)/shard_map/while/body/eval_jaxpr/all_gather | solution.py:190
  1437.3 155.6 %reduce-scatter.14.cloned.1.call-start = ((), (), s32[]{:S(2)}) async-start(), calls=%async_computation.16 | async-start | bytes 2703360 | tf_op jit(solution)/shard_map/while/body/eval_jaxpr/reduce_scatter | solution.py:199
  1598.4 30.8 %all-gather.11.cloned.1.call-start = ((), (), s32[]{:S(2)}) async-start(), calls=%async_computation.10 | async-start | bytes 1351680 | tf_op jit(solution)/shard_map/while/body/eval_jaxpr/all_gather | solution.py:122
  1601.2 136.6 %reduce-scatter.10.cloned.1.call-start = ((), (), s32[]{:S(2)}) async-start(), calls=%async_computation.11 | async-start | bytes 2703360 | tf_op jit(solution)/shard_map/while/body/eval_jaxpr/reduce_scatter | solution.py:124
  1693.2 76.2 %all-gather.13.cloned.1.call-start = ((), (), s32[]{:S(2)}) async-start(), calls=%async_computation.12 | async-start | bytes 1351680 | tf_op jit(solution)/shard_map/while/body/eval_jaxpr/all_gather | solution.py:131
  1741.4 57.4 %all-gather.15.cloned.1.call-start = ((), (), s32[]{:S(2)}) async-start(), calls=%async_computation.13 | async-start | bytes 1351680 | tf_op jit(solution)/shard_map/while/body/eval_jaxpr/all_gather | solution.py:174
  1742.6 15.8 collective-permute-start.1
  1760.9 92.4 %reduce-scatter.12.cloned.1.call-start = ((), (), s32[]{:S(2)}) async-start(), calls=%async_computation.14 | async-start | bytes 2703360 | tf_op jit(solution)/shard_map/while/body/eval_jaxpr/reduce_scatter | solution.py:182
  1808.7 78.6 %all-gather.17.cloned.1.call-start = ((), (), s32[]{:S(2)}) async-start(), calls=%async_computation.15 | async-start | bytes 1351680 | tf_op jit(solution)/shard_map/while/body/eval_jaxpr/all_gather | solution.py:190
  1859.3 155.6 %reduce-scatter.14.cloned.1.call-start = ((), (), s32[]{:S(2)}) async-start(), calls=%async_computation.16 | async-start | bytes 2703360 | tf_op jit(solution)/shard_map/while/body/eval_jaxpr/reduce_scatter | solution.py:199
  2022.2 197.2 %all-reduce.39.cloned.1.call-start = ((), (), s32[]{:S(2)}) async-start(), calls=%async_computation.5 | async-start | bytes 21233664 | tf_op jit(solution)/shard_map/psum | solution.py:347
  2028.9 34.6 %copy-start.124 = (f32[2,192]{1,0:T(2,128)S(1)}, f32[2,192]{1,0:T(2,128)}, u32[]{:S(2)}) copy-start(f32[2,192]{1,0:T(2,128)} %get-tuple-element.559) | copy-start | bytes 4612
  (386 other events, 2580.7 us)
Sparse Core Ops, SparseCore 0:
  67.3 30.7 all-gather.6
  157.2 44.4 reduce-scatter.5
  204.1 27.8 all-gather.8
  238.7 44.4 reduce-scatter.7
  302.6 29.0 all-gather.6
  390.9 44.4 reduce-scatter.5
  437.7 27.8 all-gather.8
  472.3 44.4 reduce-scatter.7
  536.2 29.0 all-gather.6
  624.5 44.4 reduce-scatter.5
  671.3 27.8 all-gather.8
  706.0 44.4 reduce-scatter.7
  757.0 27.8 all-gather.10
  849.1 44.4 reduce-scatter.9
  897.3 27.8 all-gather.12
  926.6 27.9 all-gather.14
  964.6 44.4 reduce-scatter.11
  1015.2 27.8 all-gather.16
  1126.2 44.4 reduce-scatter.13
  1179.1 27.8 all-gather.10
  1271.1 44.4 reduce-scatter.9
  1319.4 27.8 all-gather.12
  1348.8 27.9 all-gather.14
  1386.8 44.4 reduce-scatter.11
  1437.4 27.8 all-gather.16
  1548.4 44.4 reduce-scatter.13
  1601.3 27.8 all-gather.10
  1693.3 44.4 reduce-scatter.9
  1741.6 27.8 all-gather.12
  1770.9 27.9 all-gather.14
  1808.8 44.4 reduce-scatter.11
  1859.4 27.8 all-gather.16
  1970.4 44.4 reduce-scatter.13
Sparse Core Ops, SparseCore 1:
  2029.0 190.3 all-reduce.38
where the time goes:
time: 2250 us; the launch traced here: 2240 us
  waiting for transfers between devices  1230 us (55%)
  matrix products  430 us (19%)
  local copies, waits for them, and re-layouts  279 us (12%)
  other arithmetic  208 us (9%)
  blocking collectives  46.2 us (2%)
    reduce_scatter x6, waiting for transfers between devices, run_layer(): lax.psum_scatter(jnp.dot(mixed_low, w_out, preferred_element_type=jnp.flo...  261 us
    all_gather x6, waiting for transfers between devices, run_layer(): lax.all_gather(normed.astype(jnp.bfloat16), 'tensor', axis=0, tiled=True)  166 us
    psum x1, waiting for transfers between devices, per_device(): lax.psum((sum_in, sum_short, sum_cond, sum_spec, sum_gain, sum_out, sum_g...  143 us
    reduce_scatter x3, waiting for transfers between devices, run_layer(): lax.psum_scatter(jnp.dot(act_low, w_down, preferred_element_type=jnp.floa...  134 us
    reduce_scatter x3, waiting for transfers between devices, back_layer(): lax.psum_scatter(jnp.einsum('lf,df->ld', piece, w_gate_up, preferred_elem...  134 us
    dot_general x9, matrix products, orchid_mix(): jnp.dot(inverse_table, joined, precision=highest)  124 us
    dot_general x9, matrix products, orchid_mix(): jnp.dot(forward_table, pieces, precision=highest)  123 us
    all_gather x6, waiting for transfers between devices, run_layer(): lax.all_gather(normed_two.astype(jnp.bfloat16), 'tensor', axis=0, tiled=T...  110 us
  transfers between devices with their start and end apart: 40, of which 40 were waited for; matrix products, arithmetic and copies ran while one was open for 5% of the time, Pallas kernels for 0%

commit v1 on v0

--- a/solution.py
+++ b/solution.py
@@ -187,7 +187,12 @@
     )
     grad_hidden_part, grad_gain_two = norm_pull_two(grad_normed_two)
     grad_hidden = grad_out + grad_hidden_part
-    grad_mix_rows = lax.all_gather(grad_hidden.astype(jnp.bfloat16), "tensor", axis=0, tiled=True)
+    grad_mix_rows = jnp.concatenate(
+        lax.all_to_all(
+            jnp.stack([grad_hidden.astype(jnp.bfloat16)] * lax.axis_size("tensor")), "tensor", 0, 0
+        ),
+        axis=0,
+    )
     grad_mixed = jnp.einsum("ld,cd->lc", grad_mix_rows, w_out, preferred_element_type=jnp.float32)
     grad_w_out = jnp.einsum(
         "lc,ld->cd", mixed_low, grad_mix_rows, preferred_element_type=jnp.float32

time: 2250 us -> 2250 us (level)
    all_gather x3 -> x0, waiting for transfers between devices: 59.9 us -> none  [back_layer(): lax.all_gather(grad_hidden.astype(jnp.bfloat16), 'tensor', axis=0, tiled=...]
    all_to_all x0 -> x3, waiting for transfers between devices: none -> 55.6 us  [back_layer(): lax.all_to_all(jnp.stack([grad_hidden.astype(jnp.bfloat16)] * lax.axis_si...]
    while x750 -> x744, local copies, waits for them, and re-layouts: 61.9 us -> 59.3 us
where the time goes in v1:
time: 2250 us
  waiting for transfers between devices  1220 us (54%)
  matrix products  436 us (19%)
  local copies, waits for them, and re-layouts  280 us (12%)
  other arithmetic  206 us (9%)
  blocking collectives  46.2 us (2%)
  starting transfers between devices  29.6 us (1%)
    reduce_scatter x6, waiting for transfers between devices, run_layer(): lax.psum_scatter(jnp.dot(mixed_low, w_out, preferred_element_type=jnp.flo...  261 us
    all_gather x6, waiting for transfers between devices, run_layer(): lax.all_gather(normed.astype(jnp.bfloat16), 'tensor', axis=0, tiled=True)  166 us
    psum x1, waiting for transfers between devices, per_device(): lax.psum((sum_in, sum_short, sum_cond, sum_spec, sum_gain, sum_out, sum_g...  143 us
    reduce_scatter x3, waiting for transfers between devices, back_layer(): lax.psum_scatter(jnp.einsum('lf,df->ld', piece, w_gate_up, preferred_elem...  134 us
    reduce_scatter x3, waiting for transfers between devices, run_layer(): lax.psum_scatter(jnp.dot(act_low, w_down, preferred_element_type=jnp.floa...  134 us
    dot_general x9, matrix products, orchid_mix(): jnp.dot(inverse_table, joined, precision=highest)  124 us
    dot_general x9, matrix products, orchid_mix(): jnp.dot(forward_table, pieces, precision=highest)  123 us
    all_gather x6, waiting for transfers between devices, run_layer(): lax.all_gather(normed_two.astype(jnp.bfloat16), 'tensor', axis=0, tiled=T...  110 us
  transfers between devices with their start and end apart: 40, of which 40 were waited for; matrix products, arithmetic and copies ran while one was open for 5% of the time, Pallas kernels for 0%

profile of v1, /device:TPU:0, one launch (start us, length us, event | category | flops | bytes accessed | tf_op | source)
XLA Modules:
  0.0 2245.5 jit_solution(2205921302178640751)
XLA Ops:
  48.2 704.5 %while.51 = (s32[]{:T(128)}, f32[176,768]{1,0:T(8,128)S(1)}, f32[2,176,768]{2,1,0:T(8,128)S(1)}, f32[2,176,768]{2,1,0:T(8,128)}, pred[]{:T(512)}, /*index=5*/s32...) while((s32[]{:T(128)}, f32[176,768]{1,0:T(8,128)S(1)}, ...), condition=%wide.region_8.9_spmd.clone, body=%wide.region_0.8_spmd.clone.sunk | while | flops 23922319360 | bytes 190306960 | solution.py:288
  67.5 30.6 %all-gather.6.cloned.1.call-done = bf16[704,768]{1,0:T(8,128)(2,1)} async-done(((bf16[176,768]{1,0:T(8,128)(2,1)}), bf16[704,768]{1,0:T(8,128)(2,1)}) %all-gather.6.cloned.1.call-update) | async-done | bytes 1081360 | tf_op jit(solution)/shard_map/while/body/eval_jaxpr/all_gather | solution.py:122
  113.5 13.8 convolution_bitcast_fusion.15
  136.2 13.9 fusion.255
  157.9 43.8 %reduce-scatter.6.cloned.1.call-done = f32[176,768]{1,0:T(8,128)} async-done(((f32[704,768]{1,0:T(8,128)}), f32[176,768]{1,0:T(8,128)}) %reduce-scatter.6.cloned.1.call-update) | async-done | bytes 540688 | tf_op jit(solution)/shard_map/while/body/eval_jaxpr/reduce_scatter | solution.py:124
  204.1 27.9 %all-gather.8.cloned.1.call-done = bf16[704,768]{1,0:T(8,128)(2,1)} async-done(((bf16[176,768]{1,0:T(8,128)(2,1)}), bf16[704,768]{1,0:T(8,128)(2,1)}) %all-gather.8.cloned.1.call-update) | async-done | bytes 1081360 | tf_op jit(solution)/shard_map/while/body/eval_jaxpr/all_gather | solution.py:131
  238.7 44.6 %reduce-scatter.8.cloned.1.call-done = f32[176,768]{1,0:T(8,128)} async-done(((f32[704,768]{1,0:T(8,128)}), f32[176,768]{1,0:T(8,128)}) %reduce-scatter.8.cloned.1.call-update) | async-done | bytes 540688 | tf_op jit(solution)/shard_map/while/body/eval_jaxpr/reduce_scatter | solution.py:147
  302.8 28.9 %all-gather.6.cloned.1.call-done = bf16[704,768]{1,0:T(8,128)(2,1)} async-done(((bf16[176,768]{1,0:T(8,128)(2,1)}), bf16[704,768]{1,0:T(8,128)(2,1)}) %all-gather.6.cloned.1.call-update) | async-done | bytes 1081360 | tf_op jit(solution)/shard_map/while/body/eval_jaxpr/all_gather | solution.py:122
  347.2 13.8 convolution_bitcast_fusion.15
  369.9 13.9 fusion.255
  391.6 43.8 %reduce-scatter.6.cloned.1.call-done = f32[176,768]{1,0:T(8,128)} async-done(((f32[704,768]{1,0:T(8,128)}), f32[176,768]{1,0:T(8,128)}) %reduce-scatter.6.cloned.1.call-update) | async-done | bytes 540688 | tf_op jit(solution)/shard_map/while/body/eval_jaxpr/reduce_scatter | solution.py:124
  437.8 27.9 %all-gather.8.cloned.1.call-done = bf16[704,768]{1,0:T(8,128)(2,1)} async-done(((bf16[176,768]{1,0:T(8,128)(2,1)}), bf16[704,768]{1,0:T(8,128)(2,1)}) %all-gather.8.cloned.1.call-update) | async-done | bytes 1081360 | tf_op jit(solution)/shard_map/while/body/eval_jaxpr/all_gather | solution.py:131
  472.3 44.6 %reduce-scatter.8.cloned.1.call-done = f32[176,768]{1,0:T(8,128)} async-done(((f32[704,768]{1,0:T(8,128)}), f32[176,768]{1,0:T(8,128)}) %reduce-scatter.8.cloned.1.call-update) | async-done | bytes 540688 | tf_op jit(solution)/shard_map/while/body/eval_jaxpr/reduce_scatter | solution.py:147
  536.5 28.9 %all-gather.6.cloned.1.call-done = bf16[704,768]{1,0:T(8,128)(2,1)} async-done(((bf16[176,768]{1,0:T(8,128)(2,1)}), bf16[704,768]{1,0:T(8,128)(2,1)}) %all-gather.6.cloned.1.call-update) | async-done | bytes 1081360 | tf_op jit(solution)/shard_map/while/body/eval_jaxpr/all_gather | solution.py:122
  603.5 13.9 fusion.255
  625.2 43.8 %reduce-scatter.6.cloned.1.call-done = f32[176,768]{1,0:T(8,128)} async-done(((f32[704,768]{1,0:T(8,128)}), f32[176,768]{1,0:T(8,128)}) %reduce-scatter.6.cloned.1.call-update) | async-done | bytes 540688 | tf_op jit(solution)/shard_map/while/body/eval_jaxpr/reduce_scatter | solution.py:124
  671.4 27.9 %all-gather.8.cloned.1.call-done = bf16[704,768]{1,0:T(8,128)(2,1)} async-done(((bf16[176,768]{1,0:T(8,128)(2,1)}), bf16[704,768]{1,0:T(8,128)(2,1)}) %all-gather.8.cloned.1.call-update) | async-done | bytes 1081360 | tf_op jit(solution)/shard_map/while/body/eval_jaxpr/all_gather | solution.py:131
  706.0 44.6 %reduce-scatter.8.cloned.1.call-done = f32[176,768]{1,0:T(8,128)} async-done(((f32[704,768]{1,0:T(8,128)}), f32[176,768]{1,0:T(8,128)}) %reduce-scatter.8.cloned.1.call-update) | async-done | bytes 540688 | tf_op jit(solution)/shard_map/while/body/eval_jaxpr/reduce_scatter | solution.py:147
  753.8 1277.0 %while.52 = (s32[]{:T(128)}, f32[176,768]{1,0:T(8,128)}, f32[2,176,768]{2,1,0:T(8,128)}, f32[768]{0:T(1024)}, f32[768]{0:T(1024)}, /*index=5*/f32[768,576]{0,1:T...) while((s32[]{:T(128)}, f32[176,768]{1,0:T(8,128)}, ...), condition=%wide.region_39.40_spmd.clone, body=%wide.region_9.39_spmd.clone.sunk | while | flops 50368700416 | bytes 602126912 | solution.py:348
  759.2 25.9 %all-gather.10.cloned.1.call-done = bf16[704,768]{1,0:T(8,128)(2,1)} async-done(((bf16[176,768]{1,0:T(8,128)(2,1)}), bf16[704,768]{1,0:T(8,128)(2,1)}) %all-gather.10.cloned.1.call-update) | async-done | bytes 1081360 | tf_op jit(solution)/shard_map/while/body/eval_jaxpr/all_gather | solution.py:122
  826.7 13.9 fusion.299
  850.5 43.3 %reduce-scatter.10.cloned.1.call-done = f32[176,768]{1,0:T(8,128)} async-done(((f32[704,768]{1,0:T(8,128)}), f32[176,768]{1,0:T(8,128)}) %reduce-scatter.10.cloned.1.call-update) | async-done | bytes 540688 | tf_op jit(solution)/shard_map/while/body/eval_jaxpr/reduce_scatter | solution.py:124
  898.8 14.4 collective-permute-done.1
  931.3 23.5 %all-gather.14.cloned.1.call-done = bf16[704,768]{1,0:T(8,128)(2,1)} async-done(((bf16[176,768]{1,0:T(8,128)(2,1)}), bf16[704,768]{1,0:T(8,128)(2,1)}) %all-gather.14.cloned.1.call-update) | async-done | bytes 1081360 | tf_op jit(solution)/shard_map/while/body/eval_jaxpr/all_gather | solution.py:174
  964.7 44.6 %reduce-scatter.12.cloned.1.call-done = f32[176,768]{1,0:T(8,128)} async-done(((f32[704,768]{1,0:T(8,128)}), f32[176,768]{1,0:T(8,128)}) %reduce-scatter.12.cloned.1.call-update) | async-done | bytes 540688 | tf_op jit(solution)/shard_map/while/body/eval_jaxpr/reduce_scatter | solution.py:182
  1028.0 18.5 all-to-all-done
  1088.4 14.8 convolution_bitcast_fusion.20
  1148.3 25.2 %reduce-scatter.14.cloned.1.call-done = f32[176,768]{1,0:T(8,128)} async-done(((f32[704,768]{1,0:T(8,128)}), f32[176,768]{1,0:T(8,128)}) %reduce-scatter.14.cloned.1.call-update) | async-done | bytes 540688 | tf_op jit(solution)/shard_map/while/body/eval_jaxpr/reduce_scatter | solution.py:204
  1184.0 25.9 %all-gather.10.cloned.1.call-done = bf16[704,768]{1,0:T(8,128)(2,1)} async-done(((bf16[176,768]{1,0:T(8,128)(2,1)}), bf16[704,768]{1,0:T(8,128)(2,1)}) %all-gather.10.cloned.1.call-update) | async-done | bytes 1081360 | tf_op jit(solution)/shard_map/while/body/eval_jaxpr/all_gather | solution.py:122
  1251.5 13.9 fusion.299
  1275.3 43.2 %reduce-scatter.10.cloned.1.call-done = f32[176,768]{1,0:T(8,128)} async-done(((f32[704,768]{1,0:T(8,128)}), f32[176,768]{1,0:T(8,128)}) %reduce-scatter.10.cloned.1.call-update) | async-done | bytes 540688 | tf_op jit(solution)/shard_map/while/body/eval_jaxpr/reduce_scatter | solution.py:124
  1324.6 14.5 collective-permute-done.1
  1356.1 23.6 %all-gather.14.cloned.1.call-done = bf16[704,768]{1,0:T(8,128)(2,1)} async-done(((bf16[176,768]{1,0:T(8,128)(2,1)}), bf16[704,768]{1,0:T(8,128)(2,1)}) %all-gather.14.cloned.1.call-update) | async-done | bytes 1081360 | tf_op jit(solution)/shard_map/while/body/eval_jaxpr/all_gather | solution.py:174
  1389.6 44.6 %reduce-scatter.12.cloned.1.call-done = f32[176,768]{1,0:T(8,128)} async-done(((f32[704,768]{1,0:T(8,128)}), f32[176,768]{1,0:T(8,128)}) %reduce-scatter.12.cloned.1.call-update) | async-done | bytes 540688 | tf_op jit(solution)/shard_map/while/body/eval_jaxpr/reduce_scatter | solution.py:182
  1452.9 18.6 all-to-all-done
  1513.3 14.8 convolution_bitcast_fusion.20
  1576.2 22.3 reduce-scatter.14.cloned.1.call-done
  1608.9 25.9 %all-gather.10.cloned.1.call-done = bf16[704,768]{1,0:T(8,128)(2,1)} async-done(((bf16[176,768]{1,0:T(8,128)(2,1)}), bf16[704,768]{1,0:T(8,128)(2,1)}) %all-gather.10.cloned.1.call-update) | async-done | bytes 1081360 | tf_op jit(solution)/shard_map/while/body/eval_jaxpr/all_gather | solution.py:122
  1676.5 13.9 fusion.299
  1700.2 43.2 %reduce-scatter.10.cloned.1.call-done = f32[176,768]{1,0:T(8,128)} async-done(((f32[704,768]{1,0:T(8,128)}), f32[176,768]{1,0:T(8,128)}) %reduce-scatter.10.cloned.1.call-update) | async-done | bytes 540688 | tf_op jit(solution)/shard_map/while/body/eval_jaxpr/reduce_scatter | solution.py:124
  1749.6 14.5 collective-permute-done.1
  1781.1 23.6 %all-gather.14.cloned.1.call-done = bf16[704,768]{1,0:T(8,128)(2,1)} async-done(((bf16[176,768]{1,0:T(8,128)(2,1)}), bf16[704,768]{1,0:T(8,128)(2,1)}) %all-gather.14.cloned.1.call-update) | async-done | bytes 1081360 | tf_op jit(solution)/shard_map/while/body/eval_jaxpr/all_gather | solution.py:174
  1814.6 44.6 %reduce-scatter.12.cloned.1.call-done = f32[176,768]{1,0:T(8,128)} async-done(((f32[704,768]{1,0:T(8,128)}), f32[176,768]{1,0:T(8,128)}) %reduce-scatter.12.cloned.1.call-update) | async-done | bytes 540688 | tf_op jit(solution)/shard_map/while/body/eval_jaxpr/reduce_scatter | solution.py:182
  1877.8 18.6 all-to-all-done
  1938.3 14.8 convolution_bitcast_fusion.20
  2001.1 22.3 reduce-scatter.14.cloned.1.call-done
  2038.3 33.8 %all-reduce.34 = (f32[1,768]{1,0:T(1,128)}, f32[1,768]{1,0:T(1,128)}) all-reduce(f32[1,768]{1,0:T(1,128)S(1)} %broadcast_in_dim.232, f32[1,768]{1,0:T(1,128)S(1)} %broadcast_in_dim.237), channel_id=1, replica_groups=mesh['section'=2,'dp'=4,'tensor'=4] {'dp','tensor'}, use_global_device_ids=true, to_apply=%region_40.41 | all-reduce | flops 1536 | bytes 12288 | tf_op jit(solution)/shard_map/psum | solution.py:356
  2084.6 143.4 %all-reduce.39.cloned.1.call-done = (f32[1,768,3,192]{1,3,2,0:T(8,128)}, f32[1,2,705,192]{2,3,1,0:T(8,128)}, f32[1,192,768]{2,1,0:T(8,128)}, f32[1,768,2,768]{3,2,1,0:T(2,128)}, f32[1,768,768]{2,1,0:T(8,128)}) async-done(((f32[1,768,3,192]{1,3,2,0:T(8,128)}, f32[1,2,705,192]{2,3,1,0:T(8,128)}, f32[1,192,768]{2,1,0:T(8,128)}, f32[1,768,2,768]{3,2,1,0:T(2,128)}, f32[1,768,768]{2,1,0:T(8,128)}), ...) | async-done | bytes 10520080 | tf_op jit(solution)/shard_map/psum | solution.py:352
  (1301 shorter events, 865.1 us)
Async XLA Ops:
  48.4 49.6 %all-gather.6.cloned.1.call-start = ((), (), s32[]{:S(2)}) async-start(), calls=%async_computation.7 | async-start | bytes 1351680 | tf_op jit(solution)/shard_map/while/body/eval_jaxpr/all_gather | solution.py:122
  48.5 16.4 collective-permute-start
  67.2 134.6 %reduce-scatter.6.cloned.1.call-start = ((), (), s32[]{:S(2)}) async-start(), calls=%async_computation.8 | async-start | bytes 2703360 | tf_op jit(solution)/shard_map/while/body/eval_jaxpr/reduce_scatter | solution.py:124
  157.2 74.9 %all-gather.8.cloned.1.call-start = ((), (), s32[]{:S(2)}) async-start(), calls=%async_computation.9 | async-start | bytes 1351680 | tf_op jit(solution)/shard_map/while/body/eval_jaxpr/all_gather | solution.py:131
  204.1 79.2 %reduce-scatter.8.cloned.1.call-start = ((), (), s32[]{:S(2)}) async-start(), calls=%async_computation.10 | async-start | bytes 2703360 | tf_op jit(solution)/shard_map/while/body/eval_jaxpr/reduce_scatter | solution.py:147
  238.6 44.6 %copy-start.41 = (f32[2,176,768]{2,1,0:T(8,128)S(1)}, f32[2,176,768]{2,1,0:T(8,128)}, u32[]{:S(2)}) copy-start(f32[2,176,768]{2,1,0:T(8,128)} %get-tuple-element.1576) | copy-start | bytes 3244036 | tf_op jit(solution)/shard_map/while
  285.4 46.3 %all-gather.6.cloned.1.call-start = ((), (), s32[]{:S(2)}) async-start(), calls=%async_computation.7 | async-start | bytes 1351680 | tf_op jit(solution)/shard_map/while/body/eval_jaxpr/all_gather | solution.py:122
  285.5 14.7 collective-permute-start
  302.5 132.9 %reduce-scatter.6.cloned.1.call-start = ((), (), s32[]{:S(2)}) async-start(), calls=%async_computation.8 | async-start | bytes 2703360 | tf_op jit(solution)/shard_map/while/body/eval_jaxpr/reduce_scatter | solution.py:124
  390.8 74.9 %all-gather.8.cloned.1.call-start = ((), (), s32[]{:S(2)}) async-start(), calls=%async_computation.9 | async-start | bytes 1351680 | tf_op jit(solution)/shard_map/while/body/eval_jaxpr/all_gather | solution.py:131
  437.7 79.2 %reduce-scatter.8.cloned.1.call-start = ((), (), s32[]{:S(2)}) async-start(), calls=%async_computation.10 | async-start | bytes 2703360 | tf_op jit(solution)/shard_map/while/body/eval_jaxpr/reduce_scatter | solution.py:147
  472.3 44.6 %copy-start.41 = (f32[2,176,768]{2,1,0:T(8,128)S(1)}, f32[2,176,768]{2,1,0:T(8,128)}, u32[]{:S(2)}) copy-start(f32[2,176,768]{2,1,0:T(8,128)} %get-tuple-element.1576) | copy-start | bytes 3244036 | tf_op jit(solution)/shard_map/while
  519.1 46.3 %all-gather.6.cloned.1.call-start = ((), (), s32[]{:S(2)}) async-start(), calls=%async_computation.7 | async-start | bytes 1351680 | tf_op jit(solution)/shard_map/while/body/eval_jaxpr/all_gather | solution.py:122
  519.1 14.7 collective-permute-start
  536.2 132.9 %reduce-scatter.6.cloned.1.call-start = ((), (), s32[]{:S(2)}) async-start(), calls=%async_computation.8 | async-start | bytes 2703360 | tf_op jit(solution)/shard_map/while/body/eval_jaxpr/reduce_scatter | solution.py:124
  624.5 74.9 %all-gather.8.cloned.1.call-start = ((), (), s32[]{:S(2)}) async-start(), calls=%async_computation.9 | async-start | bytes 1351680 | tf_op jit(solution)/shard_map/while/body/eval_jaxpr/all_gather | solution.py:131
  671.4 79.2 %reduce-scatter.8.cloned.1.call-start = ((), (), s32[]{:S(2)}) async-start(), calls=%async_computation.10 | async-start | bytes 2703360 | tf_op jit(solution)/shard_map/while/body/eval_jaxpr/reduce_scatter | solution.py:147
  706.0 44.6 %copy-start.41 = (f32[2,176,768]{2,1,0:T(8,128)S(1)}, f32[2,176,768]{2,1,0:T(8,128)}, u32[]{:S(2)}) copy-start(f32[2,176,768]{2,1,0:T(8,128)} %get-tuple-element.1576) | copy-start | bytes 3244036 | tf_op jit(solution)/shard_map/while
  754.3 33.3 %copy-start.5 = (f32[2,176,768]{2,1,0:T(8,128)}, f32[2,176,768]{2,1,0:T(8,128)S(1)}, u32[]{:S(2)}) copy-start(f32[2,176,768]{2,1,0:T(8,128)S(1)} %get-tuple-element.1720) | copy-start | bytes 3244036 | tf_op jit(solution)/shard_map/while
  754.3 33.3 %copy-start.58 = (s32[2,704]{1,0:T(2,128)}, s32[2,704]{1,0:T(2,128)S(1)}, u32[]{:S(2)}) copy-start(s32[2,704]{1,0:T(2,128)S(1)} %get-tuple-element.1724) | copy-start | bytes 16900 | tf_op jit(solution)/shard_map/while
  754.3 33.3 %copy-start.85 = (f32[1,768]{1,0:T(1,128)}, f32[1,768]{1,0:T(1,128)S(1)}, u32[]{:S(2)}) copy-start(f32[1,768]{1,0:T(1,128)S(1)} %get-tuple-element.1722) | copy-start | bytes 9220 | tf_op jit(solution)/shard_map/while
  754.3 30.8 %all-gather.10.cloned.1.call-start = ((), (), s32[]{:S(2)}) async-start(), calls=%async_computation.11 | async-start | bytes 1351680 | tf_op jit(solution)/shard_map/while/body/eval_jaxpr/all_gather | solution.py:122
  757.1 136.7 %reduce-scatter.10.cloned.1.call-start = ((), (), s32[]{:S(2)}) async-start(), calls=%async_computation.12 | async-start | bytes 2703360 | tf_op jit(solution)/shard_map/while/body/eval_jaxpr/reduce_scatter | solution.py:124
  849.1 76.3 %all-gather.12.cloned.1.call-start = ((), (), s32[]{:S(2)}) async-start(), calls=%async_computation.13 | async-start | bytes 1351680 | tf_op jit(solution)/shard_map/while/body/eval_jaxpr/all_gather | solution.py:131
  897.4 57.4 %all-gather.14.cloned.1.call-start = ((), (), s32[]{:S(2)}) async-start(), calls=%async_computation.14 | async-start | bytes 1351680 | tf_op jit(solution)/shard_map/while/body/eval_jaxpr/all_gather | solution.py:174
  897.5 15.8 collective-permute-start.1
  915.8 93.5 %reduce-scatter.12.cloned.1.call-start = ((), (), s32[]{:S(2)}) async-start(), calls=%async_computation.15 | async-start | bytes 2703360 | tf_op jit(solution)/shard_map/while/body/eval_jaxpr/reduce_scatter | solution.py:182
  1015.6 30.8 %all-to-all-start = ((bf16[4,176,768]{2,1,0:T(8,128)(2,1)}), bf16[4,176,768]{2,1,0:T(8,128)(2,1)}, u32[]{:S(2)}, u32[]{:S(2)}) async-start(bf16[4,176,768]{2,1,0:T(8,128)(2,1)} %stack.4), calls=%async_computation.4 | async-start | bytes 2162688 | tf_op jit(solution)/shard_map/while/body/eval_jaxpr/all_to_all | solution.py:191
  1019.9 153.6 %reduce-scatter.14.cloned.1.call-start = ((), (), s32[]{:S(2)}) async-start(), calls=%async_computation.16 | async-start | bytes 2703360 | tf_op jit(solution)/shard_map/while/body/eval_jaxpr/reduce_scatter | solution.py:204
  1142.0 34.3 %copy-start.106 = (f32[3,192]{1,0:T(4,128)}, f32[3,192]{1,0:T(4,128)S(1)}, u32[]{:S(2)}) copy-start(f32[3,192]{1,0:T(4,128)S(1)} %select_add_fusion.22) | copy-start | bytes 6916 | tf_op jit(solution)/shard_map/while
  1179.1 30.7 %all-gather.10.cloned.1.call-start = ((), (), s32[]{:S(2)}) async-start(), calls=%async_computation.11 | async-start | bytes 1351680 | tf_op jit(solution)/shard_map/while/body/eval_jaxpr/all_gather | solution.py:122
  1181.9 136.6 %reduce-scatter.10.cloned.1.call-start = ((), (), s32[]{:S(2)}) async-start(), calls=%async_computation.12 | async-start | bytes 2703360 | tf_op jit(solution)/shard_map/while/body/eval_jaxpr/reduce_scatter | solution.py:124
  1273.9 76.3 %all-gather.12.cloned.1.call-start = ((), (), s32[]{:S(2)}) async-start(), calls=%async_computation.13 | async-start | bytes 1351680 | tf_op jit(solution)/shard_map/while/body/eval_jaxpr/all_gather | solution.py:131
  1322.2 57.6 %all-gather.14.cloned.1.call-start = ((), (), s32[]{:S(2)}) async-start(), calls=%async_computation.14 | async-start | bytes 1351680 | tf_op jit(solution)/shard_map/while/body/eval_jaxpr/all_gather | solution.py:174
  1323.3 15.8 collective-permute-start.1
  1341.6 92.6 %reduce-scatter.12.cloned.1.call-start = ((), (), s32[]{:S(2)}) async-start(), calls=%async_computation.15 | async-start | bytes 2703360 | tf_op jit(solution)/shard_map/while/body/eval_jaxpr/reduce_scatter | solution.py:182
  1440.6 30.9 %all-to-all-start = ((bf16[4,176,768]{2,1,0:T(8,128)(2,1)}), bf16[4,176,768]{2,1,0:T(8,128)(2,1)}, u32[]{:S(2)}, u32[]{:S(2)}) async-start(bf16[4,176,768]{2,1,0:T(8,128)(2,1)} %stack.4), calls=%async_computation.4 | async-start | bytes 2162688 | tf_op jit(solution)/shard_map/while/body/eval_jaxpr/all_to_all | solution.py:191
  1444.8 153.7 %reduce-scatter.14.cloned.1.call-start = ((), (), s32[]{:S(2)}) async-start(), calls=%async_computation.16 | async-start | bytes 2703360 | tf_op jit(solution)/shard_map/while/body/eval_jaxpr/reduce_scatter | solution.py:204
  1604.1 30.8 %all-gather.10.cloned.1.call-start = ((), (), s32[]{:S(2)}) async-start(), calls=%async_computation.11 | async-start | bytes 1351680 | tf_op jit(solution)/shard_map/while/body/eval_jaxpr/all_gather | solution.py:122
  1606.8 136.6 %reduce-scatter.10.cloned.1.call-start = ((), (), s32[]{:S(2)}) async-start(), calls=%async_computation.12 | async-start | bytes 2703360 | tf_op jit(solution)/shard_map/while/body/eval_jaxpr/reduce_scatter | solution.py:124
  1698.9 76.3 %all-gather.12.cloned.1.call-start = ((), (), s32[]{:S(2)}) async-start(), calls=%async_computation.13 | async-start | bytes 1351680 | tf_op jit(solution)/shard_map/while/body/eval_jaxpr/all_gather | solution.py:131
  1747.1 57.6 %all-gather.14.cloned.1.call-start = ((), (), s32[]{:S(2)}) async-start(), calls=%async_computation.14 | async-start | bytes 1351680 | tf_op jit(solution)/shard_map/while/body/eval_jaxpr/all_gather | solution.py:174
  1748.3 15.8 collective-permute-start.1
  1766.6 92.6 %reduce-scatter.12.cloned.1.call-start = ((), (), s32[]{:S(2)}) async-start(), calls=%async_computation.15 | async-start | bytes 2703360 | tf_op jit(solution)/shard_map/while/body/eval_jaxpr/reduce_scatter | solution.py:182
  1865.5 30.9 %all-to-all-start = ((bf16[4,176,768]{2,1,0:T(8,128)(2,1)}), bf16[4,176,768]{2,1,0:T(8,128)(2,1)}, u32[]{:S(2)}, u32[]{:S(2)}) async-start(bf16[4,176,768]{2,1,0:T(8,128)(2,1)} %stack.4), calls=%async_computation.4 | async-start | bytes 2162688 | tf_op jit(solution)/shard_map/while/body/eval_jaxpr/all_to_all | solution.py:191
  1869.8 153.7 %reduce-scatter.14.cloned.1.call-start = ((), (), s32[]{:S(2)}) async-start(), calls=%async_computation.16 | async-start | bytes 2703360 | tf_op jit(solution)/shard_map/while/body/eval_jaxpr/reduce_scatter | solution.py:204
  2030.8 197.2 %all-reduce.39.cloned.1.call-start = ((), (), s32[]{:S(2)}) async-start(), calls=%async_computation.6 | async-start | bytes 21233664 | tf_op jit(solution)/shard_map/psum | solution.py:352
  2037.5 34.6 %copy-start.123 = (f32[2,192]{1,0:T(2,128)S(1)}, f32[2,192]{1,0:T(2,128)}, u32[]{:S(2)}) copy-start(f32[2,192]{1,0:T(2,128)} %get-tuple-element.559) | copy-start | bytes 4612
  (383 other events, 2625.5 us)
Sparse Core Ops, SparseCore 0:
  67.3 30.7 all-gather.5
  157.3 44.4 reduce-scatter.5
  204.2 27.8 all-gather.7
  238.8 44.4 reduce-scatter.7
  302.6 29.0 all-gather.5
  390.9 44.4 reduce-scatter.5
  437.8 27.8 all-gather.7
  472.4 44.4 reduce-scatter.7
  536.3 29.0 all-gather.5
  624.6 44.4 reduce-scatter.5
  671.5 27.8 all-gather.7
  706.1 44.4 reduce-scatter.7
  757.2 27.8 all-gather.9
  849.3 44.4 reduce-scatter.9
  897.5 27.8 all-gather.11
  926.8 27.9 all-gather.13
  964.8 44.4 reduce-scatter.11
  1129.5 43.9 reduce-scatter.13
  1182.0 27.8 all-gather.9
  1274.1 44.4 reduce-scatter.9
  1322.3 27.8 all-gather.11
  1351.8 27.9 all-gather.13
  1389.7 44.4 reduce-scatter.11
  1554.5 43.9 reduce-scatter.13
  1607.0 27.8 all-gather.9
  1699.0 44.4 reduce-scatter.9
  1747.3 27.8 all-gather.11
  1776.7 27.9 all-gather.13
  1814.7 44.4 reduce-scatter.11
  1979.4 43.9 reduce-scatter.13
Sparse Core Ops, SparseCore 1:
  2037.6 190.3 all-reduce.38
